TPU v7x, 768 devices: a whole 4x8x12 slice. The times are simulated.
768 devices in a mesh: section: 2 (over core), node: 8 (over y_lo, x), dev: 48 (over z, y_hi).
Axes of the slice: x: 4, y: 8 (y_hi: 4, y_lo: 2; y = y_hi * 2 + y_lo), z: 12, core: 2. Of those that a mesh axis runs over, the one named last changes fastest.
Arguments:
- inputs_forward: bfloat16 [2, 6144, 3584], P('section', 'dev', 'node'), may hold values from -6 to 6
- routes_forward: int32 [2, 6144, 2], P('section', 'dev'), may hold values from 0 to 47, all different within a row; in each aligned block of 128 rows (0 to 127, 128 to 255, ..., all dimensions but the last counted through in order) at most 10 rows name the same one
- gates_forward: float32 [2, 6144, 2], P('section', 'dev'), may hold values from 0.2 to 1.2
- grads_backward: bfloat16 [2, 6144, 3584], P('section', 'dev', 'node'), may hold values from -6 to 6
- routes_backward: int32 [2, 6144, 2], P('section', 'dev'), may hold values from 0 to 47, all different within a row; in each aligned block of 128 rows (0 to 127, 128 to 255, ..., all dimensions but the last counted through in order) at most 10 rows name the same one
- gates_backward: float32 [2, 6144, 2], P('section', 'dev'), may hold values from 0.2 to 1.2
- w_gate: bfloat16 [2, 48, 3584, 1024], P('section', 'dev', 'node'), may hold values from -0.09375 to 0.09375
- w_up: bfloat16 [2, 48, 3584, 1024], P('section', 'dev', 'node'), may hold values from -0.09375 to 0.09375
- w_down: bfloat16 [2, 48, 1024, 3584], P('section', 'dev', None, 'node'), may hold values from -0.1875 to 0.1875
- saved_gate: bfloat16 [2, 48, 480, 1024], P('section', 'dev'), may hold values from -5 to 5
- saved_up: bfloat16 [2, 48, 480, 1024], P('section', 'dev'), may hold values from -5 to 5
Outputs:
- forward_next: bfloat16 [2, 6144, 3584], P('section', 'dev', 'node')
- backward_next: bfloat16 [2, 6144, 3584], P('section', 'dev', 'node')
Inputs may be any that keep to these rules, and one draw needn't show every extreme that they name: `routes_forward`: each row names 2 different experts. Among the rows of one device no expert is named more than 10 times, a bound that some block reaches. `routes_backward`: each row names 2 different experts. Among the rows of one device no expert is named more than 10 times, a bound that some block reaches.
All inputs are finite; a program needn't handle non-finite values.
Results may differ from a plain program's by a relative error of at most 0.014.
Values may be sent and summed in bfloat16 or wider, within the bound.
A program may use at most 32 MiB of HBM per device.

v0:
```python
import jax
import jax.numpy as jnp
from jax import lax
from jax.sharding import PartitionSpec as P


def from_behind(value, axis, steps):
    count = lax.axis_size(axis)
    pairs = [(source, (source + steps) % count) for source in range(count)]
    return lax.ppermute(value, axis, pairs)


def slot_targets(routing, experts, capacity):
    flat = routing.reshape(-1)
    onehot = (flat[:, None] == jnp.arange(experts, dtype=jnp.int32)[None, :]).astype(jnp.int32)
    earlier = jnp.cumsum(onehot, axis=0) - onehot
    return flat * capacity + jnp.sum(earlier * onehot, axis=1)


def pack_rows(token_rows, targets, slot_count, chosen):
    match = (jnp.arange(slot_count, dtype=jnp.int32)[:, None] == targets[None, :]).astype(
        jnp.bfloat16
    )
    select = jnp.sum(match.reshape(slot_count, token_rows.shape[0], chosen), axis=2)
    return jnp.dot(select, token_rows, preferred_element_type=jnp.float32).astype(jnp.bfloat16)


def combine_rows(token_rows, weights_of, returned_rows, targets):
    width = token_rows.shape[1]
    picked = returned_rows.reshape(-1, width)[targets]
    picked = picked.reshape(token_rows.shape[0], weights_of.shape[1], width).astype(jnp.float32)
    mixed = token_rows.astype(jnp.float32) + jnp.sum(weights_of[:, :, None] * picked, axis=1)
    return mixed.astype(jnp.bfloat16)


def backward_act(grad_hidden, stored_gate, stored_up):
    act_gate = stored_gate.astype(jnp.float32)
    act_up = stored_up.astype(jnp.float32)
    squash = jax.nn.sigmoid(act_gate)
    grad_gate = (grad_hidden * act_up * squash * (1.0 + act_gate * (1.0 - squash))).astype(
        jnp.bfloat16
    )
    grad_up = (grad_hidden * act_gate * squash).astype(jnp.bfloat16)
    return (grad_gate, grad_up)


def shards(
    inputs_forward,
    routes_forward,
    gates_forward,
    grads_backward,
    routes_backward,
    gates_backward,
    w_gate,
    w_up,
    w_down,
    saved_gate,
    saved_up,
):
    experts = lax.axis_size("dev")
    chosen = routes_forward.shape[2]
    token_rows = inputs_forward[0]
    grad_rows = grads_backward[0]
    slot_total = saved_gate.shape[2]
    capacity = slot_total // experts
    width = token_rows.shape[1]
    targets_forward = slot_targets(routes_forward[0], experts, capacity)
    targets_backward = slot_targets(routes_backward[0], experts, capacity)
    sent_forward = pack_rows(token_rows, targets_forward, slot_total, chosen).reshape(
        experts, capacity, width
    )
    sent_backward = pack_rows(grad_rows, targets_backward, slot_total, chosen).reshape(
        experts, capacity, width
    )
    arrived_forward, arrived_backward = (
        lax.all_to_all(sent_forward, "dev", split_axis=0, concat_axis=0, tiled=True),
        lax.all_to_all(sent_backward, "dev", split_axis=0, concat_axis=0, tiled=True),
    )
    arrived_forward = arrived_forward.reshape(slot_total, width)
    arrived_backward = arrived_backward.reshape(slot_total, width)
    gate_local = w_gate[0, 0]
    up_local = w_up[0, 0]
    down_local = w_down[0, 0]
    stored_gate = saved_gate[0, 0]
    stored_up = saved_up[0, 0]
    contract_last = (((1,), (1,)), ((), ()))
    part_gate = jnp.dot(arrived_forward, gate_local, preferred_element_type=jnp.float32)
    part_up = jnp.dot(arrived_forward, up_local, preferred_element_type=jnp.float32)
    part_grad = lax.dot_general(
        arrived_backward, down_local, contract_last, preferred_element_type=jnp.float32
    )
    gate_share, up_share, grad_share = (
        lax.psum_scatter(
            part_gate.astype(jnp.bfloat16), "node", scatter_dimension=1, tiled=True
        ).astype(jnp.float32),
        lax.psum_scatter(
            part_up.astype(jnp.bfloat16), "node", scatter_dimension=1, tiled=True
        ).astype(jnp.float32),
        lax.psum_scatter(
            part_grad.astype(jnp.bfloat16), "node", scatter_dimension=1, tiled=True
        ).astype(jnp.float32),
    )
    share_width = gate_share.shape[1]
    offset = lax.axis_index("node") * share_width
    stored_gate_share = lax.dynamic_slice_in_dim(stored_gate, offset, share_width, 1)
    stored_up_share = lax.dynamic_slice_in_dim(stored_up, offset, share_width, 1)
    hidden_share = (jax.nn.silu(gate_share) * up_share).astype(jnp.bfloat16)
    grad_gate_share, grad_up_share = backward_act(grad_share, stored_gate_share, stored_up_share)
    hidden, grad_gate, grad_up = (
        lax.all_gather(hidden_share, "node", axis=1, tiled=True),
        lax.all_gather(grad_gate_share, "node", axis=1, tiled=True),
        lax.all_gather(grad_up_share, "node", axis=1, tiled=True),
    )
    result_forward = jnp.dot(hidden, down_local, preferred_element_type=jnp.float32).astype(
        jnp.bfloat16
    )
    result_backward = lax.dot_general(
        grad_gate, gate_local, contract_last, preferred_element_type=jnp.float32
    )
    result_backward = result_backward + lax.dot_general(
        grad_up, up_local, contract_last, preferred_element_type=jnp.float32
    )
    result_backward = result_backward.astype(jnp.bfloat16)
    back_forward, back_backward = (
        lax.all_to_all(
            result_forward.reshape(experts, capacity, width),
            "dev",
            split_axis=0,
            concat_axis=0,
            tiled=True,
        ),
        lax.all_to_all(
            result_backward.reshape(experts, capacity, width),
            "dev",
            split_axis=0,
            concat_axis=0,
            tiled=True,
        ),
    )
    mixed_forward = combine_rows(token_rows, gates_forward[0], back_forward, targets_forward)
    mixed_backward = combine_rows(grad_rows, gates_backward[0], back_backward, targets_backward)
    next_forward = from_behind(mixed_forward[None], "section", 1)
    next_backward = from_behind(mixed_backward[None], "section", -1)
    return (next_forward, next_backward)


def solution(mesh):
    return jax.shard_map(
        shards,
        mesh=mesh,
        in_specs=(
            P("section", "dev", "node"),
            P("section", "dev", None),
            P("section", "dev", None),
            P("section", "dev", "node"),
            P("section", "dev", None),
            P("section", "dev", None),
            P("section", "dev", "node", None),
            P("section", "dev", "node", None),
            P("section", "dev", None, "node"),
            P("section", "dev", None, None),
            P("section", "dev", None, None),
        ),
        out_specs=(P("section", "dev", "node"), P("section", "dev", "node")),
        check_vma=False,
    )
```

profile of v0, /device:TPU:1, one launch (start us, length us, event | category | flops | bytes accessed | tf_op | source)
XLA Modules:
  0.0 341.9 jit_solution(12107817435031372330)
XLA Ops:
  7.2 0.9 copy.53
  8.1 0.1 eq.79
  8.2 0.1 eq.83
  8.4 0.6 reduce-window.14
  9.0 0.2 slice_reduce_fusion.1
  9.3 0.1 reduce_sum.73
  9.6 1.2 convolution_convert_fusion.5
  10.8 0.2 copy.58
  11.0 0.2 reshape.175
  11.3 54.5 %all_to_all.20 = bf16[48,10,448]{2,1,0:T(8,128)(2,1)S(1)} all-to-all(bf16[48,10,448]{2,1,0:T(8,128)(2,1)S(1)} %reshape.175), channel_id=1, replica_groups=mesh['section'=2,'node'=8,'dev'=48] {'dev'}, dimensions={0} | all-to-all | bytes 860160 | tf_op jit(solution)/shard_map/all_to_all | solution.py:76
  65.7 0.3 reshape.176
  66.1 0.7 convolution_convert_fusion.1
  66.8 1.3 copy.73
  68.3 0.1 eq.90
  68.4 0.1 eq.94
  68.6 0.6 reduce-window.16
  69.2 0.2 slice_reduce_fusion
  69.5 0.1 reduce_sum.79
  69.7 0.7 convolution_convert_fusion.2
  70.4 1.3 copy.71
  72.0 0.7 copy-done.2
  72.6 0.3 convolution_convert_fusion.3
  72.9 0.2 copy.67
  73.1 0.2 reshape.180
  73.3 41.1 %all_to_all.21 = bf16[48,10,448]{2,1,0:T(8,128)(2,1)S(1)} all-to-all(bf16[48,10,448]{2,1,0:T(8,128)(2,1)S(1)} %reshape.180), channel_id=1, replica_groups=mesh['section'=2,'node'=8,'dev'=48] {'dev'}, dimensions={0} | all-to-all | bytes 860160 | tf_op jit(solution)/shard_map/all_to_all | solution.py:77
  114.4 0.3 reshape.181
  114.7 0.7 convolution_convert_fusion
  115.4 1.3 copy.75
  116.8 0.1 copy.51
  117.0 0.1 mul.101
  117.2 0.2 copy-done.4
  117.6 1.1 copy.74
  118.6 48.6 %reduce-scatter.10.cloned.1.call-done = bf16[128,480]{1,0:T(8,128)(2,1)} async-done(((bf16[1024,480]{1,0:T(8,128)(2,1)}), bf16[128,480]{1,0:T(8,128)(2,1)}) %reduce-scatter.10.cloned.1.call-update) | async-done | bytes 122896
  167.2 1.0 copy.72
  168.3 22.7 %all_gather.9 = bf16[480,1024]{1,0:T(8,128)(2,1)S(1)} all-gather(bf16[480,128]{1,0:T(8,128)(2,1)S(1)} %fusion.27), channel_id=1, replica_groups=mesh['section'=2,'node'=8,'dev'=48] {'node'}, dimensions={1}, use_global_device_ids=true | all-gather | bytes 1105920 | tf_op jit(solution)/shard_map/all_gather | solution.py:110
  191.0 0.7 convolution_convert_fusion.4
  191.7 0.2 copy.59
  191.9 1.1 reshape.177
  193.0 15.0 %all-to-all-start.1 = ((bf16[48,10,448]{2,1,0:T(8,128)(2,1)}), bf16[48,10,448]{2,1,0:T(8,128)(2,1)S(1)}, u32[]{:S(2)}, u32[]{:S(2)}) async-start(bf16[48,10,448]{2,1,0:T(8,128)(2,1)} %reshape.177), calls=%async_computation.1 | async-start | bytes 1572864 | tf_op jit(solution)/shard_map/all_to_all | solution.py:125
  208.0 10.5 %reduce-scatter.14.cloned.1.call-done = bf16[128,480]{1,0:T(8,128)(2,1)} async-done(((bf16[1024,480]{1,0:T(8,128)(2,1)}), bf16[128,480]{1,0:T(8,128)(2,1)}) %reduce-scatter.14.cloned.1.call-update) | async-done | bytes 122896
  218.6 1.1 copy.76
  219.6 1.1 fusion.24
  220.7 29.8 %all_gather.10 = bf16[480,1024]{1,0:T(8,128)(2,1)S(1)} all-gather(bf16[480,128]{1,0:T(8,128)(2,1)S(1)} %get-tuple-element.7), channel_id=1, replica_groups=mesh['section'=2,'node'=8,'dev'=48] {'node'}, dimensions={1}, use_global_device_ids=true | all-gather | bytes 1105920 | tf_op jit(solution)/shard_map/all_gather | solution.py:111
  250.5 0.7 fusion.5
  251.2 23.8 %all_gather.11 = bf16[480,1024]{1,0:T(8,128)(2,1)S(1)} all-gather(bf16[480,128]{1,0:T(8,128)(2,1)S(1)} %get-tuple-element.6), channel_id=1, replica_groups=mesh['section'=2,'node'=8,'dev'=48] {'node'}, dimensions={1}, use_global_device_ids=true | all-gather | bytes 1105920 | tf_op jit(solution)/shard_map/all_gather | solution.py:112
  275.0 0.7 fusion
  275.7 0.2 copy.68
  275.9 1.1 reshape.182
  277.0 15.5 %all-to-all-start.3 = ((bf16[48,10,448]{2,1,0:T(8,128)(2,1)}), bf16[48,10,448]{2,1,0:T(8,128)(2,1)S(1)}, u32[]{:S(2)}, u32[]{:S(2)}) async-start(bf16[48,10,448]{2,1,0:T(8,128)(2,1)} %reshape.182), calls=%async_computation.3 | async-start | bytes 1572864 | tf_op jit(solution)/shard_map/all_to_all | solution.py:132
  292.5 0.1 mul.115
  292.8 0.3 reshape.178
  293.1 1.2 gather_fusion
  294.3 0.3 reshape.184
  294.6 0.7 multiply_reduce_fusion.1
  295.4 13.0 %collective-permute-start = (bf16[1,128,448]{2,1,0:T(8,128)(2,1)S(1)}, bf16[1,128,448]{2,1,0:T(8,128)(2,1)S(1)}, u32[]{:S(2)}, u32[]{:S(2)}) collective-permute-start(bf16[1,128,448]{2,1,0:T(8,128)(2,1)S(1)} %fusion.11), channel_id=1, source_target_pairs={{0,384},{384,0},{1,385},{385,1},{2,386},{386,2},{3,387},{387,3},{4... | collective-permute-start | bytes 344072 | tf_op jit(solution)/shard_map/ppermute | solution.py:10
  308.3 7.9 %all-to-all-done.3 = bf16[48,10,448]{2,1,0:T(8,128)(2,1)S(1)} async-done(((bf16[48,10,448]{2,1,0:T(8,128)(2,1)}), bf16[48,10,448]{2,1,0:T(8,128)(2,1)S(1)}, u32[]{:S(2)}, u32[]{:S(2)}) %all-to-all-start.3) | async-done | bytes 430112 | tf_op jit(solution)/shard_map/all_to_all | solution.py:132
  316.2 0.3 reshape.183
  316.6 1.2 gather_fusion.1
  317.7 0.3 reshape.187
  318.1 0.7 multiply_reduce_fusion
  318.8 14.8 %collective-permute-start.1 = (bf16[1,128,448]{2,1,0:T(8,128)(2,1)S(1)}, bf16[1,128,448]{2,1,0:T(8,128)(2,1)S(1)}, u32[]{:S(2)}, u32[]{:S(2)}) collective-permute-start(bf16[1,128,448]{2,1,0:T(8,128)(2,1)S(1)} %fusion.10), channel_id=1, source_target_pairs={{0,384},{384,0},{1,385},{385,1},{2,386},{386,2},{3,387},{387,3},{4... | collective-permute-start | bytes 344072 | tf_op jit(solution)/shard_map/ppermute | solution.py:10
  333.7 0.8 copy.69
  334.4 0.2 collective-permute-done.1
  334.6 0.8 copy.70
  (54 shorter events, 1.5 us)
Async XLA Ops:
  7.2 107.5 %copy-start = (bf16[1,1,1024,448]{2,3,1,0:T(8,128)(2,1)S(1)}, bf16[1,1,1024,448]{2,3,1,0:T(8,128)(2,1)}, u32[]{:S(2)}) copy-start(bf16[1,1,1024,448]{2,3,1,0:T(8,128)(2,1)} %param.19) | copy-start | bytes 2752516
  7.2 110.4 %reduce-scatter.12.cloned.1.call-start = ((), (), s32[]{:S(2)}) async-start(), calls=%async_computation.8 | async-start | bytes 1179648
  11.2 54.8 %copy-start.8 = (bf16[1,1,448,1024]{3,2,1,0:T(8,128)(2,1)S(1)}, bf16[1,1,448,1024]{3,2,1,0:T(8,128)(2,1)}, u32[]{:S(2)}) copy-start(bf16[1,1,448,1024]{3,2,1,0:T(8,128)(2,1)} %param.18) | copy-start | bytes 2752516
  66.7 1.4 copy-start.3
  68.1 1.6 copy-start.6
  68.1 99.1 %reduce-scatter.10.cloned.1.call-start = ((), (), s32[]{:S(2)}) async-start(), calls=%async_computation.7 | async-start | bytes 1179648
  71.7 0.9 copy-start.2
  71.7 146.8 %reduce-scatter.14.cloned.1.call-start = ((), (), s32[]{:S(2)}) async-start(), calls=%async_computation.9 | async-start | bytes 1179648
  115.4 1.4 copy-start.1
  116.7 0.7 copy-start.4
  193.0 83.9 %all-to-all-start.1 = ((bf16[48,10,448]{2,1,0:T(8,128)(2,1)}), bf16[48,10,448]{2,1,0:T(8,128)(2,1)S(1)}, u32[]{:S(2)}, u32[]{:S(2)}) async-start(bf16[48,10,448]{2,1,0:T(8,128)(2,1)} %reshape.177), calls=%async_computation.1 | async-start | bytes 1572864 | tf_op jit(solution)/shard_map/all_to_all | solution.py:125
  208.0 42.5 %copy-start.7 = (bf16[1,1,448,1024]{3,2,1,0:T(8,128)(2,1)S(1)}, bf16[1,1,448,1024]{3,2,1,0:T(8,128)(2,1)}, u32[]{:S(2)}) copy-start(bf16[1,1,448,1024]{3,2,1,0:T(8,128)(2,1)} %param.17) | copy-start | bytes 2752516
  251.2 23.8 %copy-start.9 = (bf16[1,1,448,1024]{3,2,1,0:T(8,128)(2,1)S(1)}, bf16[1,1,448,1024]{3,2,1,0:T(8,128)(2,1)}, u32[]{:S(2)}) copy-start(bf16[1,1,448,1024]{3,2,1,0:T(8,128)(2,1)} %param.18) | copy-start | bytes 2752516
  277.0 15.7 %copy-start.5 = (f32[1,128,2]{1,2,0:T(2,128)S(1)}, f32[1,128,2]{1,2,0:T(2,128)}, u32[]{:S(2)}) copy-start(f32[1,128,2]{1,2,0:T(2,128)} %param.16) | copy-start | bytes 3076
  277.0 39.3 %all-to-all-start.3 = ((bf16[48,10,448]{2,1,0:T(8,128)(2,1)}), bf16[48,10,448]{2,1,0:T(8,128)(2,1)S(1)}, u32[]{:S(2)}, u32[]{:S(2)}) async-start(bf16[48,10,448]{2,1,0:T(8,128)(2,1)} %reshape.182), calls=%async_computation.3 | async-start | bytes 1572864 | tf_op jit(solution)/shard_map/all_to_all | solution.py:132
  295.4 38.3 %collective-permute-start = (bf16[1,128,448]{2,1,0:T(8,128)(2,1)S(1)}, bf16[1,128,448]{2,1,0:T(8,128)(2,1)S(1)}, u32[]{:S(2)}, u32[]{:S(2)}) collective-permute-start(bf16[1,128,448]{2,1,0:T(8,128)(2,1)S(1)} %fusion.11), channel_id=1, source_target_pairs={{0,384},{384,0},{1,385},{385,1},{2,386},{386,2},{3,387},{387,3},{4... | collective-permute-start | bytes 344072 | tf_op jit(solution)/shard_map/ppermute | solution.py:10
  318.8 15.8 %collective-permute-start.1 = (bf16[1,128,448]{2,1,0:T(8,128)(2,1)S(1)}, bf16[1,128,448]{2,1,0:T(8,128)(2,1)S(1)}, u32[]{:S(2)}, u32[]{:S(2)}) collective-permute-start(bf16[1,128,448]{2,1,0:T(8,128)(2,1)S(1)} %fusion.10), channel_id=1, source_target_pairs={{0,384},{384,0},{1,385},{385,1},{2,386},{386,2},{3,387},{387,3},{4... | collective-permute-start | bytes 344072 | tf_op jit(solution)/shard_map/ppermute | solution.py:10
Sparse Core Ops, SparseCore 0:
  68.2 45.7 reduce-scatter.11
  117.1 50.0 reduce-scatter.9
  170.3 48.2 reduce-scatter.13
where the time goes:
time: 343 us; the launch traced here: 342 us
  blocking collectives  172 us (50%)
  waiting for transfers between devices  67.3 us (20%)
  starting transfers between devices  58.4 us (17%)
  local copies, waits for them, and re-layouts  20.3 us (6%)
  between operations  14.2 us (4%)
  matrix products  5.53 us (2%)
  other arithmetic  4.38 us (1%)
    unnamed x6, waiting for transfers between devices  59.2 us
    all_to_all x1, blocking collectives, shards(): lax.all_to_all(sent_forward, 'dev', split_axis=0, concat_axis=0, tiled=True)  54.5 us
    all_to_all x1, blocking collectives, shards(): lax.all_to_all(sent_backward, 'dev', split_axis=0, concat_axis=0, tiled=T...  41.1 us
    all_gather x1, blocking collectives, shards(): lax.all_gather(grad_gate_share, 'node', axis=1, tiled=True)  29.8 us
    ppermute x2, starting transfers between devices, from_behind(): return lax.ppermute(value, axis, pairs)  27.8 us
    all_gather x1, blocking collectives, shards(): lax.all_gather(grad_up_share, 'node', axis=1, tiled=True)  23.8 us
    all_gather x1, blocking collectives, shards(): lax.all_gather(hidden_share, 'node', axis=1, tiled=True)  22.7 us
    all_to_all x1, starting transfers between devices, shards(): lax.all_to_all(result_backward.reshape(experts, capacity, width), 'dev',...  15.5 us
  transfers between devices with their start and end apart: 7, of which 4 were waited for; matrix products, arithmetic and copies ran while one was open for 6% of the time, Pallas kernels for 0%

commit v1 on v0

v1 whole, which is shorter than its diff:
```python
import functools

import jax
import jax.numpy as jnp
from jax import lax
from jax.experimental import pallas as pl
from jax.experimental.pallas import tpu as pltpu
from jax.sharding import PartitionSpec as P

MESH = pl.DeviceIdType.MESH
BF, F32 = jnp.bfloat16, jnp.float32
HEAD, TAIL = 8, 2
CAPACITY = HEAD + TAIL
NODES = 8
NT = (((1,), (1,)), ((), ()))
TN = (((0,), (0,)), ((), ()))


def dot(left, right, dims=(((1,), (0,)), ((), ()))):
    return lax.dot_general(left, right, dims, preferred_element_type=F32)


def columns_of(routes, experts):
    tokens = routes.shape[0]
    lane = lax.broadcasted_iota(jnp.int32, (tokens, experts), 1)
    named = [routes[:, k : k + 1] == lane for k in range(2)]
    both = jnp.where(named[0] | named[1], 1.0, 0.0).astype(BF)
    before = lax.broadcasted_iota(jnp.int32, (tokens, tokens), 0) > lax.broadcasted_iota(
        jnp.int32, (tokens, tokens), 1
    )
    count = dot(jnp.where(before, 1.0, 0.0).astype(BF), both)
    found = []
    for k in range(2):
        rank = jnp.sum(jnp.where(named[k], count, 0.0), axis=1, keepdims=True).astype(jnp.int32)
        expert = routes[:, k : k + 1]
        head = jnp.where(rank < HEAD, expert * HEAD + rank, -1)
        tail = jnp.where(rank >= HEAD, expert * TAIL + rank - HEAD, -1)
        found.append((head, tail))
    return found


def onehot(column, width):
    lane = lax.broadcasted_iota(jnp.int32, (column.shape[0], width), 1)
    return jnp.where(column == lane, 1.0, 0.0).astype(BF)


def peer_of(me, k, planes, lanes):
    return ((me // lanes + k // lanes) % planes) * lanes + (me % lanes + k % lanes) % lanes


def drain(ref, sem):
    pltpu.make_async_copy(ref, ref, sem).wait()


def kernel(
    experts, sections, tokf, tokb, rf, rb, gf, gb, wg_h, wu_h, wd_h, sg_h, su_h, outf, outb,
    wg, wu, wd, sg, su, sgp, sup, sa, sb, ra, rbuf, part, got, sums, hid, ca, cb, da, db, osend, orecv,
    load_sem, own_sem, disp_s, disp_r, ret_s, ret_r, red_s, red_r, gat_s, gat_r, sec_s, sec_r,
):
    me = lax.axis_index("dev")
    node = lax.axis_index("node")
    section = lax.axis_index("section")
    lanes = 4 if experts % 4 == 0 else 1
    planes = experts // lanes
    x = node % 4
    bit_y, bit_1 = node // 4, x // 2
    bit_0 = (x + x // 2) % 2
    partner = {
        0: (node // 4) * 4 + x + 1 - 2 * (x % 2),
        1: (node // 4) * 4 + 3 - x,
        2: (node + 4) % 8,
    }
    block = bit_y * 4 + bit_1 * 2 + bit_0

    barrier = pltpu.get_barrier_semaphore()

    def greet(k, carry):
        pl.semaphore_signal(
            barrier, inc=1, device_id={"dev": peer_of(me, k, planes, lanes)}, device_id_type=MESH
        )
        return carry

    lax.fori_loop(1, experts, greet, 0)
    for d in range(3):
        pl.semaphore_signal(barrier, inc=1, device_id={"node": partner[d]}, device_id_type=MESH)
    pl.semaphore_signal(barrier, inc=1, device_id={"section": 1 - section}, device_id_type=MESH)

    share = pl.ds(pl.multiple_of(block * 128, 128), 128)
    loads = [
        pltpu.make_async_copy(wg_h, wg, load_sem.at[0]),
        pltpu.make_async_copy(wu_h, wu, load_sem.at[1]),
        pltpu.make_async_copy(wd_h, wd, load_sem.at[2]),
        pltpu.make_async_copy(sg_h.at[:, share], sg, load_sem.at[3]),
        pltpu.make_async_copy(su_h.at[:, share], su, load_sem.at[4]),
    ]
    for load in loads:
        load.start()

    for m, (tok, routes) in enumerate(((tokf, rf), (tokb, rb))):
        (h0, t0), (h1, t1) = columns_of(routes[...], experts)
        pick_head = onehot(h0, experts * HEAD) + onehot(h1, experts * HEAD)
        pick_tail = onehot(t0, experts * TAIL) + onehot(t1, experts * TAIL)
        rows = tok[...]
        width = rows.shape[1]
        sa[m] = dot(pick_head, rows, TN).astype(BF).reshape(experts, HEAD, width)
        sb[m] = dot(pick_tail, rows, TN).astype(BF).reshape(experts, TAIL, width)

    pl.semaphore_wait(barrier, experts - 1 + 4)

    def exchange(src_a, src_b, dst_a, dst_b, send, recv, m):
        def go(k, carry):
            p = peer_of(me, k, planes, lanes)
            for i, (src, dst) in enumerate(((src_a, dst_a), (src_b, dst_b))):
                pltpu.make_async_remote_copy(
                    src_ref=src.at[m, p],
                    dst_ref=dst.at[m, me],
                    send_sem=send.at[m, i],
                    recv_sem=recv.at[m, i],
                    device_id={"dev": p},
                    device_id_type=MESH,
                ).start()
            return carry

        lax.fori_loop(1, experts, go, 0)

    def keep(src_a, src_b, dst_a, dst_b, m):
        own = [
            pltpu.make_async_copy(src_a.at[m, me], dst_a.at[m, me], own_sem.at[0]),
            pltpu.make_async_copy(src_b.at[m, me], dst_b.at[m, me], own_sem.at[1]),
        ]
        for c in own:
            c.start()
        for c in own:
            c.wait()

    def settle(dst_a, dst_b, sems, m):
        drain(dst_a.at[m, pl.ds(0, experts - 1)], sems.at[m, 0])
        drain(dst_b.at[m, pl.ds(0, experts - 1)], sems.at[m, 1])

    exchange(sa, sb, ra, rbuf, disp_s, disp_r, 0)
    exchange(sa, sb, ra, rbuf, disp_s, disp_r, 1)
    keep(sa, sb, ra, rbuf, 0)
    keep(sa, sb, ra, rbuf, 1)

    for load in loads:
        load.wait()
    slots = experts * CAPACITY
    new = lax.broadcasted_iota(jnp.int32, (slots, 1), 0)
    late = new - experts * HEAD
    old = jnp.where(
        new < experts * HEAD,
        (new // HEAD) * CAPACITY + new % HEAD,
        (late // TAIL) * CAPACITY + HEAD + late % TAIL,
    )
    order = onehot(old, slots)
    sgp[...] = dot(order, sg[...])
    sup[...] = dot(order, su[...])

    half = slots // 2
    span = [pl.ds(0, half), pl.ds(half, half)]
    bits = {0: bit_0, 1: bit_1, 2: bit_y}

    def at(c, y, second, first):
        return y * 4 + (second * 2 + first if c == 0 else first * 2 + second)

    def axes(c):
        return (0, 1) if c == 0 else (1, 0)

    def remote(src, dst, send, recv, to):
        return pltpu.make_async_remote_copy(
            src_ref=src, dst_ref=dst, send_sem=send, recv_sem=recv,
            device_id={"node": partner[to]}, device_id_type=MESH,
        )

    def arrived_rows(a, b, m):
        return jnp.concatenate(
            [
                a[m].reshape(experts * HEAD, a.shape[-1]),
                b[m].reshape(experts * TAIL, b.shape[-1]),
            ],
            axis=0,
        )

    def partial(t, m, w, transposed):
        rows = arrived_rows(ra, rbuf, m)
        for j in range(4):
            if transposed:
                y = dot(rows, w[j * 256 : (j + 1) * 256, :], NT)
            else:
                y = dot(rows, w[:, j * 256 : (j + 1) * 256])
            y = y.astype(BF)
            part[t, 2 * j] = y[:, :128]
            part[t, 2 * j + 1] = y[:, 128:]

    def red_copy(t, c, i):
        d1, d2 = axes(c)
        n1, n2, ny = 1 - bits[d1], bits[d2], bits[2]
        if i < 4:
            second = 1 - n2 if i < 2 else n2
            y = 1 - ny if i % 2 == 0 else ny
            src, to = part.at[t, at(c, y, second, n1), span[c]], d1
        else:
            src, to = sums.at[t, c, i - 4], (d2 if i < 6 else 2)
        return remote(src, got.at[t, c, i], red_s.at[t, c, i], red_r.at[t, c, i], to)

    def mine(t, c, y, second):
        d1, _ = axes(c)
        return part[t, at(c, y, second, bits[d1]), span[c]].astype(F32)

    def red_start(t):
        for i in range(4):
            for c in range(2):
                red_copy(t, c, i).start()

    def red_a(t, i):
        for c in range(2):
            _, d2 = axes(c)
            red_copy(t, c, i).wait_recv()
            y = 1 - bits[2] if i == 0 else bits[2]
            value = mine(t, c, y, 1 - bits[d2]) + got[t, c, i].astype(F32)
            sums[t, c, i] = value.astype(BF)
            red_copy(t, c, 4 + i).start()

    def red_c(t):
        for c in range(2):
            _, d2 = axes(c)
            red_copy(t, c, 2).wait_recv()
            red_copy(t, c, 4).wait_recv()
            value = mine(t, c, 1 - bits[2], bits[d2]) + got[t, c, 2].astype(F32)
            sums[t, c, 2] = (value + got[t, c, 4].astype(F32)).astype(BF)
            red_copy(t, c, 6).start()

    def red_d(t, c):
        _, d2 = axes(c)
        for i in (3, 5, 6):
            red_copy(t, c, i).wait_recv()
        value = mine(t, c, bits[2], bits[d2]) + got[t, c, 3].astype(F32)
        return value + got[t, c, 5].astype(F32) + got[t, c, 6].astype(F32)

    def gat_copy(t, c, i):
        d1, d2 = axes(c)
        b1, b2, by = bits[d1], bits[d2], bits[2]
        y, second, to = (
            (by, b2, 2), (by, b2, d2), (1 - by, b2, d2),
            (by, b2, d1), (1 - by, b2, d1), (by, 1 - b2, d1), (1 - by, 1 - b2, d1),
        )[i]
        ref = hid.at[t, at(c, y, second, b1), span[c]]
        return remote(ref, ref, gat_s.at[t, c, i], gat_r.at[t, c, i], to)

    def gat_start(t, c):
        for i in (0, 1, 3):
            gat_copy(t, c, i).start()

    def gat_step(t, c, wait, starts):
        gat_copy(t, c, wait).wait_recv()
        for i in starts:
            gat_copy(t, c, i).start()

    def gat_middle(t):
        for wait, starts in ((0, (2, 4)), (1, (5,)), (2, (6,))):
            for c in range(2):
                gat_step(t, c, wait, starts)

    def gat_end(t):
        for c in range(2):
            for i in range(3, 7):
                gat_copy(t, c, i).wait_recv()

    def gathered(t):
        return jnp.concatenate([hid[t, b] for b in range(NODES)], axis=1)

    def send_back(m, value):
        value = value.astype(BF)
        cut = experts * HEAD
        ca[m] = value[:cut].reshape(experts, HEAD, value.shape[1])
        cb[m] = value[cut:].reshape(experts, TAIL, value.shape[1])
        exchange(ca, cb, da, db, ret_s, ret_r, m)
        keep(ca, cb, da, db, m)

    settle(ra, rbuf, disp_r, 0)
    partial(0, 0, wg, False)
    red_start(0)
    partial(1, 0, wu, False)
    red_start(1)
    for t in (0, 1):
        red_a(t, 0)
        red_a(t, 1)
    settle(ra, rbuf, disp_r, 1)
    partial(2, 1, wd, True)
    red_start(2)
    for t in (0, 1):
        red_c(t)
    for c in range(2):
        gate, up = red_d(0, c), red_d(1, c)
        hid[0, block, span[c]] = (jax.nn.silu(gate) * up).astype(BF)
        gat_start(0, c)
    red_a(2, 0)
    red_a(2, 1)
    gat_middle(0)
    red_c(2)
    for c in range(2):
        grad = red_d(2, c)
        a, u = sgp[span[c]], sup[span[c]]
        q = jax.nn.sigmoid(a)
        hid[1, block, span[c]] = (grad * u * q * (1.0 + a * (1.0 - q))).astype(BF)
        hid[2, block, span[c]] = (grad * a * q).astype(BF)
        gat_start(1, c)
        gat_start(2, c)
    gat_end(0)
    send_back(0, dot(gathered(0), wd[...]))
    gat_middle(1)
    gat_middle(2)
    gat_end(1)
    gat_end(2)
    send_back(1, dot(gathered(1), wg[...], NT) + dot(gathered(2), wu[...], NT))

    final = []
    for m, (tok, routes, gates, out) in enumerate(((tokf, rf, gf, outf), (tokb, rb, gb, outb))):
        settle(da, db, ret_r, m)
        heads, tails = arrived_rows(da, db, m)[: experts * HEAD], arrived_rows(da, db, m)[experts * HEAD :]
        mixed = tok[...].astype(F32)
        weighted = None
        for k, (head, tail) in enumerate(columns_of(routes[...], experts)):
            picked = dot(onehot(head, experts * HEAD), heads) + dot(onehot(tail, experts * TAIL), tails)
            term = gates[:, k : k + 1] * picked
            weighted = term if weighted is None else weighted + term
        osend[m] = (mixed + weighted).astype(BF)
        copy = pltpu.make_async_remote_copy(
            src_ref=osend.at[m], dst_ref=orecv.at[m], send_sem=sec_s.at[m], recv_sem=sec_r.at[m],
            device_id={"section": 1 - section}, device_id_type=MESH,
        )
        copy.start()
        final.append((copy, out))
    for m, (copy, out) in enumerate(final):
        copy.wait_recv()
        out[...] = orecv[m]

    for m in range(2):
        settle(sa, sb, disp_s, m)
        settle(ca, cb, ret_s, m)
        final[m][0].wait_send()
    for t in range(3):
        for c in range(2):
            for i in range(7):
                red_copy(t, c, i).wait_send()
                gat_copy(t, c, i).wait_send()


def solution(mesh):
    experts, sections = mesh.shape["dev"], mesh.shape["section"]

    def shards(inf, rf, gf, inb, rb, gb, wg, wu, wd, sg, su):
        args = [v[0] for v in (inf, inb, rf, rb, gf, gb)] + [v[0, 0] for v in (wg, wu, wd, sg, su)]
        tokens, width = args[0].shape
        slots, hidden = args[9].shape
        half, share = slots // 2, hidden // NODES
        vm = lambda *shape: pltpu.VMEM(shape, BF)
        both = [vm(2, experts, HEAD, width), vm(2, experts, TAIL, width)]
        dma = pltpu.SemaphoreType.DMA
        outs = pl.pallas_call(
            functools.partial(kernel, experts, sections),
            out_shape=[jax.ShapeDtypeStruct((tokens, width), BF)] * 2,
            in_specs=[pl.BlockSpec(memory_space=pltpu.VMEM)] * 6 + [pl.BlockSpec(memory_space=pl.ANY)] * 5,
            out_specs=[pl.BlockSpec(memory_space=pltpu.VMEM)] * 2,
            scratch_shapes=[vm(width, hidden), vm(width, hidden), vm(hidden, width), vm(slots, share), vm(slots, share)]
            + [pltpu.VMEM((slots, share), F32)] * 2
            + both + both
            + [vm(3, NODES, slots, share), vm(3, 2, 7, half, share), vm(3, 2, 3, half, share), vm(3, NODES, slots, share)]
            + both + both
            + [vm(2, tokens, width)] * 2
            + [dma((5,)), dma((2,))] + [dma((2, 2))] * 4 + [dma((3, 2, 7))] * 4 + [dma((2,))] * 2,
            compiler_params=pltpu.CompilerParams(
                collective_id=0, has_side_effects=True, vmem_limit_bytes=56 * 1024 * 1024
            ),
            name="relay_layer",
        )(*args)
        return tuple(o[None] for o in outs)

    return jax.shard_map(
        shards,
        mesh=mesh,
        in_specs=(P("section", "dev", "node"), P("section", "dev", None), P("section", "dev", None)) * 2
        + (P("section", "dev", "node", None),) * 2
        + (P("section", "dev", None, "node"),)
        + (P("section", "dev", None, None),) * 2,
        out_specs=(P("section", "dev", "node"), P("section", "dev", "node")),
        check_vma=False,
    )
```

time: 343 us -> 138 us (0.40)
  blocking collectives: 172 us -> 0 us
  Pallas kernels: 0 us -> 127 us
  waiting for transfers between devices: 67.3 us -> 0 us
  starting transfers between devices: 58.4 us -> 0 us
  between operations: 14.2 us -> 0.66 us
  local copies, waits for them, and re-layouts: 20.3 us -> 10.7 us
  matrix products: 5.53 us -> 0 us
  other arithmetic: 4.38 us -> 0 us
    pallas_call x0 -> x1, Pallas kernels: none -> 127 us  [shards(): pl.pallas_call(functools.partial(kernel, experts, sections), out_shape=[j...]
    all_to_all x2 -> x0, blocking collectives: 95.5 us -> none  [the longest x1 54.5 us: shards(): lax.all_to_all(sent_forward, 'dev', split_axis=0, concat_axis=0, tiled=True)]
    all_gather x3 -> x0, blocking collectives: 76.3 us -> none  [the longest x1 29.8 us: shards(): lax.all_gather(grad_gate_share, 'node', axis=1, tiled=True)]
    unnamed x6 -> x0, waiting for transfers between devices: 59.2 us -> none
    all_to_all x2 -> x0, starting transfers between devices: 30.5 us -> none  [the longest x1 15.5 us: shards(): lax.all_to_all(result_backward.reshape(experts, capacity, width), 'dev',...]
    ppermute x2 -> x0, starting transfers between devices: 27.8 us -> none  [from_behind(): return lax.ppermute(value, axis, pairs)]
    all_to_all x2 -> x0, waiting for transfers between devices: 7.9 us -> none  [the longest x1 7.9 us: shards(): lax.all_to_all(result_backward.reshape(experts, capacity, width), 'dev',...]
    dot_general x8 -> x0, matrix products: 5.53 us -> none  [the longest x2 1.47 us: pack_rows(): jnp.dot(select, token_rows, preferred_element_type=jnp.float32)]
  transfers between devices with their start and end apart: 7 -> 0, of which waited for: 4 -> 0; matrix products, arithmetic and copies ran while one was open for 6% -> 0% of each run, Pallas kernels for 0% -> 0%
where the time goes in v1:
time: 138 us
  Pallas kernels  127 us (92%)
  local copies, waits for them, and re-layouts  10.7 us (8%)
    pallas_call x1, Pallas kernels, shards(): pl.pallas_call(functools.partial(kernel, experts, sections), out_shape=[j...  127 us
    unnamed x23, local copies, waits for them, and re-layouts  10.7 us

profile of v1, /device:TPU:1, one launch (start us, length us, event | category | flops | bytes accessed | tf_op | source)
XLA Modules:
  0.0 138.2 jit_solution(4629727428361891024)
XLA Ops:
  0.6 0.0 copy-start.3
  0.6 0.7 copy-done.3
  1.3 0.0 copy-start.4
  1.3 0.0 copy-start.5
  1.3 0.7 copy.15
  2.1 0.0 copy-start.1
  2.1 0.0 copy-done.4
  2.1 0.7 copy.17
  2.8 0.0 copy-done.5
  2.8 0.7 copy.16
  3.5 0.0 copy-start.6
  3.5 0.7 copy-done.6
  4.2 0.7 copy.18
  4.9 0.0 copy-done.1
  4.9 0.0 copy-start.2
  4.9 0.8 copy.13
  5.7 0.1 copy-done.2
  5.8 0.8 copy.14
  6.6 2.2 %copy.19 = bf16[1,1,1024,448]{3,2,1,0:T(8,128)(2,1)} copy(bf16[1,1,1024,448]{2,3,1,0:T(8,128)(2,1)} %param.19) | data formatting | bytes 1835008 | tf_op args[8]
  8.8 126.8 %relay_layer.1 = (bf16[128,448]{1,0:T(8,128)(2,1)}, bf16[128,448]{1,0:T(8,128)(2,1)}) custom-call(bf16[128,448]{1,0:T(8,128)(2,1)} %bitcast.18, bf16[128,448]{1,0:T(8,128)(2,1)} %bitcast.19, s32[128,2]{1,0:T(8,128)} %bitcast.20, s32[128,2]{1,0:T(8,128)} %bitcast.22, f32[128,2]{1,0:T(8,128)} %bitcast.21, f32[128,2]{1,0:T(8,128)} %bitcast.23, ...), custom_call_target="tpu_custom_call" | custom-call | tf_op jit(solution)/shard_map/relay_layer/pallas_call | solution.py:360
  135.7 0.0 copy-start
  135.7 1.7 %copy.20 = bf16[1,128,448]{1,2,0:T(8,128)(2,1)} copy(bf16[1,128,448]{2,1,0:T(8,128)(2,1)} %bitcast.25) | data formatting | bytes 229376
  137.4 0.0 copy-done
  137.4 0.8 copy.21
Async XLA Ops:
  0.6 0.7 copy-start.3
  1.3 0.7 copy-start.4
  1.3 1.5 %copy-start.5 = (s32[1,128,2]{1,2,0:T(2,128)S(1)}, s32[1,128,2]{1,2,0:T(2,128)}, u32[]{:S(2)}) copy-start(s32[1,128,2]{1,2,0:T(2,128)} %param.15) | copy-start | bytes 3076
  2.1 2.9 %copy-start.1 = (bf16[1,128,448]{1,2,0:T(8,128)(2,1)S(1)}, bf16[1,128,448]{1,2,0:T(8,128)(2,1)}, u32[]{:S(2)}) copy-start(bf16[1,128,448]{1,2,0:T(8,128)(2,1)} %param.11) | copy-start | bytes 344068
  3.5 0.7 copy-start.6
  4.9 0.9 copy-start.2
  135.7 1.7 %copy-start = (bf16[128,448]{1,0:T(8,128)(2,1)S(1)}, bf16[128,448]{1,0:T(8,128)(2,1)}, u32[]{:S(2)}) copy-start(bf16[128,448]{1,0:T(8,128)(2,1)} %get-tuple-element.5) | copy-start | bytes 344068

commit v2 on v1

v2 whole, which is shorter than its diff:
```python
import functools

import jax
import jax.numpy as jnp
from jax import lax
from jax.experimental import pallas as pl
from jax.experimental.pallas import tpu as pltpu
from jax.sharding import PartitionSpec as P

MESH = pl.DeviceIdType.MESH
BF, F32 = jnp.bfloat16, jnp.float32
HEAD, TAIL = 8, 2
CAPACITY = HEAD + TAIL
NODES = 8
LANES = 4
GROUPS = ((0, 1, 11), (2, 10, 3), (6, 5, 7), (4, 8, 9))
PLANES = 12
CHUNKS = len(GROUPS)
DISTANCE = tuple(d for group in GROUPS for d in group)
NN = (((1,), (0,)), ((), ()))
NT = (((1,), (1,)), ((), ()))
TN = (((0,), (0,)), ((), ()))
PAD = 64


def dot(left, right, dims=NN):
    return lax.dot_general(left, right, dims, preferred_element_type=F32)


def table(index, values):
    found = jnp.zeros_like(index)
    for i, value in enumerate(values):
        found = jnp.where(index == i, value, found)
    return found


def iota(shape, dim):
    return lax.broadcasted_iota(jnp.int32, shape, dim)


def drain(ref, sem):
    pltpu.make_async_copy(ref, ref, sem).wait()


def widen(first, second):
    return jnp.concatenate(
        [first[:, :384], first[:, 384:] + second[:, :128], second[:, 128:]], axis=1
    ).astype(BF)


def kernel(
    experts, tokf, tokb, rf, rb, gf, gb, wg_h, wu_h, wd_h, sg_h, su_h, outf, outb,
    wg, wu, wd, sg, su, for_gate, for_up, sel, sa, sb, ra, rb_in, part, got, sums, hid, ca, cb, da, db, acc, osend, orecv,
    load_sem, own_sem, disp_s, disp_r, ret_s, ret_r, red_s, red_r, gat_s, gat_r, sec_s, sec_r,
):
    me = lax.axis_index("dev")
    node = lax.axis_index("node")
    section = lax.axis_index("section")
    z, lane = me // LANES, me % LANES
    x = node % 4
    bits = {0: (x + x // 2) % 2, 1: x // 2, 2: node // 4}
    partner = {
        0: (node // 4) * 4 + x + 1 - 2 * (x % 2),
        1: (node // 4) * 4 + 3 - x,
        2: (node + 4) % 8,
    }
    block = bits[2] * 4 + bits[1] * 2 + bits[0]
    group = experts // CHUNKS
    slots = experts * CAPACITY
    rows = slots // CHUNKS
    cut = group * HEAD

    def ahead(dz, dy):
        return ((z + dz) % PLANES) * LANES + (lane + dy) % LANES

    def behind(dz, dy):
        return ((z + PLANES - dz) % PLANES) * LANES + (lane + LANES - dy) % LANES

    barrier = pltpu.get_barrier_semaphore()

    def greet(k, carry):
        pl.semaphore_signal(
            barrier, inc=1, device_id={"dev": (me + k) % experts}, device_id_type=MESH
        )
        return carry

    lax.fori_loop(1, experts, greet, 0)
    for d in range(3):
        pl.semaphore_signal(barrier, inc=1, device_id={"node": partner[d]}, device_id_type=MESH)
    pl.semaphore_signal(barrier, inc=1, device_id={"section": 1 - section}, device_id_type=MESH)

    inner = pl.ds(PAD, wg_h.shape[0])
    for w in (wg, wu, wd):
        w[:PAD] = jnp.zeros((PAD, w.shape[1]), BF)
        w[w.shape[0] - PAD :] = jnp.zeros((PAD, w.shape[1]), BF)
    loads = [
        pltpu.make_async_copy(wg_h, wg.at[inner], load_sem.at[0]),
        pltpu.make_async_copy(wu_h, wu.at[inner], load_sem.at[1]),
        pltpu.make_async_copy(wd_h, wd.at[inner], load_sem.at[2]),
        pltpu.make_async_copy(sg_h, sg, load_sem.at[3]),
        pltpu.make_async_copy(su_h, su, load_sem.at[4]),
    ]
    for load in loads:
        load.start()
    front, back = pl.ds(0, 512), pl.ds(PAD, 512)

    tokens = rf.shape[1]
    for m, routes in enumerate((rf, rb)):
        named = [routes[k : k + 1, :] == iota((experts, tokens), 0) for k in range(2)]
        both = jnp.where(named[0] | named[1], 1.0, 0.0).astype(BF)
        earlier = jnp.where(iota((tokens, tokens), 0) < iota((tokens, tokens), 1), 1.0, 0.0)
        count = dot(both, earlier.astype(BF))
        for k in range(2):
            rank = jnp.sum(jnp.where(named[k], count, 0.0), axis=0, keepdims=True).astype(jnp.int32)
            expert = routes[k : k + 1, :]
            dz = (expert // LANES + PLANES - z) % PLANES
            dy = (expert % LANES + LANES - lane) % LANES
            place = table(dz, [DISTANCE.index(d) for d in range(PLANES)]) * LANES + dy
            chunk, local = place // group, place % group
            slot = chunk * rows + jnp.where(
                rank < HEAD, local * HEAD + rank, cut + local * TAIL + rank - HEAD
            )
            sel[m, :, k * tokens : (k + 1) * tokens] = jnp.where(
                slot == iota((slots, tokens), 0), 1.0, 0.0
            ).astype(BF)

    gap = jnp.zeros((PAD, tokens), BF)
    wide = (
        jnp.concatenate([tokf[...], gap], axis=0),
        jnp.concatenate([gap, tokb[...]], axis=0),
    )

    def split(value, head, tail, c):
        width = value.shape[1]
        ks = slice(c * group, (c + 1) * group)
        head[ks] = value[:cut].reshape(group, HEAD, width)
        tail[ks] = value[cut:].reshape(group, TAIL, width)

    def joined(head, tail, c):
        ks = slice(c * group, (c + 1) * group)
        width = head.shape[-1]
        return jnp.concatenate(
            [head[ks].reshape(cut, width), tail[ks].reshape(group * TAIL, width)], axis=0
        )

    def pack(c):
        halves = []
        for m in range(2):
            chosen = sel[m, c * rows : (c + 1) * rows, :]
            halves.append(dot(chosen[:, :tokens] + chosen[:, tokens:], wide[m], NT))
        split(widen(*halves), sa, sb, c)

    def exchange(c, pairs, send, recv, to):
        for i, dz in enumerate(GROUPS[c]):
            first = (c * len(GROUPS[c]) + i) * LANES

            def go(dy, carry, first=first, dz=dz):
                for j, (src, dst) in enumerate(pairs):
                    pltpu.make_async_remote_copy(
                        src_ref=src.at[first + dy],
                        dst_ref=dst.at[first + dy],
                        send_sem=send.at[j],
                        recv_sem=recv.at[c, j],
                        device_id={"dev": to(dz, dy)},
                        device_id_type=MESH,
                    ).start()
                return carry

            lax.fori_loop(1 if dz == 0 else 0, LANES, go, 0)
            if dz == 0:
                own = [
                    pltpu.make_async_copy(src.at[first], dst.at[first], own_sem.at[j])
                    for j, (src, dst) in enumerate(pairs)
                ]
                for copy in own:
                    copy.start()
                for copy in own:
                    copy.wait()

    def settle(c, pairs, recv):
        for j, (_, dst) in enumerate(pairs):
            drain(dst.at[pl.ds(0, group - (0 in GROUPS[c]))], recv.at[c, j])

    out_pairs = ((sa, ra), (sb, rb_in))
    back_pairs = ((ca, da), (cb, db))

    for c in range(CHUNKS):
        pack(c)
        if c == 0:
            pl.semaphore_wait(barrier, experts - 1 + 4)
        exchange(c, out_pairs, disp_s, disp_r, ahead)

    for load in loads[:3]:
        load.wait()

    def factors():
        for load in loads[3:]:
            load.wait()
        new = iota((slots, 1), 0)
        chunk, local = new // rows, new % rows
        late = local - cut
        place = chunk * group + jnp.where(local < cut, local // HEAD, late // TAIL)
        rank = jnp.where(local < cut, local % HEAD, HEAD + late % TAIL)
        dz, dy = table(place // LANES, DISTANCE), place % LANES
        old = behind(dz, dy) * CAPACITY + rank
        order = jnp.where(old == iota((slots, slots), 1), 1.0, 0.0).astype(BF)
        for j in range(4):
            span = slice(j * 256, (j + 1) * 256)
            a, u = dot(order, sg[:, span]), dot(order, su[:, span])
            q = jax.nn.sigmoid(a)
            for_gate[:, span] = u * q * (1.0 + a * (1.0 - q))
            for_up[:, span] = a * q

    def axes(t, c):
        return (0, 1) if (t + c) % 2 == 0 else (1, 0)

    def at(t, c, y, second, first):
        return y * 4 + (second * 2 + first if axes(t, c)[0] == 0 else first * 2 + second)

    def remote(src, dst, send, recv, to):
        return pltpu.make_async_remote_copy(
            src_ref=src, dst_ref=dst, send_sem=send, recv_sem=recv,
            device_id={"node": partner[to]}, device_id_type=MESH,
        )

    def red_copy(t, c, i):
        d1, d2 = axes(t, c)
        n1, n2, ny = 1 - bits[d1], bits[d2], bits[2]
        if i < 4:
            second = 1 - n2 if i < 2 else n2
            y = 1 - ny if i % 2 == 0 else ny
            src, to = part.at[t, c, at(t, c, y, second, n1)], d1
        else:
            src, to = sums.at[t, c, i - 4], (d2 if i < 6 else 2)
        return remote(src, got.at[t, c, i], red_s.at[t, c, i], red_r.at[t, c, i], to)

    def mine(t, c, y, second):
        d1, _ = axes(t, c)
        return part[t, c, at(t, c, y, second, bits[d1])].astype(F32)

    def red_start(t, c):
        for i in range(4):
            red_copy(t, c, i).start()

    def red_a(t, c, i):
        _, d2 = axes(t, c)
        red_copy(t, c, i).wait_recv()
        y = 1 - bits[2] if i == 0 else bits[2]
        value = mine(t, c, y, 1 - bits[d2]) + got[t, c, i].astype(F32)
        sums[t, c, i] = value.astype(BF)
        red_copy(t, c, 4 + i).start()

    def red_c(t, c):
        _, d2 = axes(t, c)
        red_copy(t, c, 2).wait_recv()
        red_copy(t, c, 4).wait_recv()
        value = mine(t, c, 1 - bits[2], bits[d2]) + got[t, c, 2].astype(F32)
        sums[t, c, 2] = (value + got[t, c, 4].astype(F32)).astype(BF)
        red_copy(t, c, 6).start()

    def red_d(t, c):
        _, d2 = axes(t, c)
        for i in (3, 5, 6):
            red_copy(t, c, i).wait_recv()
        value = mine(t, c, bits[2], bits[d2]) + got[t, c, 3].astype(F32)
        return value + got[t, c, 5].astype(F32) + got[t, c, 6].astype(F32)

    def gat_copy(t, c, i):
        d1, d2 = axes(t, c)
        b1, b2, by = bits[d1], bits[d2], bits[2]
        y, second, to = (
            (by, b2, 2), (by, b2, d2), (1 - by, b2, d2),
            (by, b2, d1), (1 - by, b2, d1), (by, 1 - b2, d1), (1 - by, 1 - b2, d1),
        )[i]
        ref = hid.at[t, c, at(t, c, y, second, b1)]
        return remote(ref, ref, gat_s.at[t, c, i], gat_r.at[t, c, i], to)

    def gat_start(t, c):
        for i in (0, 1, 3):
            gat_copy(t, c, i).start()

    def gathered(t, c):
        return jnp.concatenate([hid[t, c, b] for b in range(NODES)], axis=1)

    def products(c):
        settle(c, out_pairs, disp_r)
        arrived = joined(ra, rb_in, c)
        for t, (value, w, zone) in enumerate(
            ((arrived[:, :512], wg, back), (arrived[:, :512], wu, back), (arrived[:, 384:], wd, front))
        ):
            for j in range(4):
                y = dot(value, w[zone, j * 256 : (j + 1) * 256]).astype(BF)
                part[t, c, 2 * j] = y[:, :128]
                part[t, c, 2 * j + 1] = y[:, 128:]
            red_start(t, c)

    def halve(c):
        for i in range(2):
            for t in range(3):
                red_a(t, c, i)

    def settle_y(c):
        for t in range(3):
            red_c(t, c)

    def activate(c):
        gate, up = red_d(0, c), red_d(1, c)
        hid[0, c, block] = (jax.nn.silu(gate) * up).astype(BF)
        gat_start(0, c)
        hid[1, c, block] = red_d(2, c).astype(BF)
        gat_start(1, c)

    def forward(c):
        for wait, starts in ((0, (2, 4)), (1, (5,)), (2, (6,))):
            for t in range(2):
                gat_copy(t, c, wait).wait_recv()
                for i in starts:
                    gat_copy(t, c, i).start()

    def finish(c):
        for t in range(2):
            for i in range(3, 7):
                gat_copy(t, c, i).wait_recv()
        first = dot(gathered(0, c), wd[back, :], NT)
        grad = gathered(1, c).astype(F32)
        mine_rows = slice(c * rows, (c + 1) * rows)
        second = dot((grad * for_gate[mine_rows, :]).astype(BF), wg[front, :], NT)
        second = second + dot((grad * for_up[mine_rows, :]).astype(BF), wu[front, :], NT)
        split(widen(first, second), ca, cb, c)
        exchange(c, back_pairs, ret_s, ret_r, behind)

    stages = {"W": products, "A": halve, "C": settle_y, "D": activate, "G": forward, "E": finish, "F": lambda _: factors()}
    for step in ORDER:
        stages[step[0]](int(step[1]))

    for c in range(CHUNKS):
        settle(c, back_pairs, ret_r)
        returned = joined(da, db, c)
        for m in range(2):
            value = returned[:, :512] if m == 0 else returned[:, 384:]
            picked = dot(value, sel[m, c * rows : (c + 1) * rows, :], TN)
            acc[m] = picked if c == 0 else acc[m] + picked
    final = []
    for m, (tok, gates, out) in enumerate(((tokf, gf, outf), (tokb, gb, outb))):
        picked = acc[m, : 512 - PAD, :] if m == 0 else acc[m, PAD:, :]
        weighted = gates[0:1, :] * picked[:, :tokens] + gates[1:2, :] * picked[:, tokens:]
        osend[m] = (tok[...].astype(F32) + weighted).astype(BF)
        copy = pltpu.make_async_remote_copy(
            src_ref=osend.at[m], dst_ref=orecv.at[m], send_sem=sec_s.at[m], recv_sem=sec_r.at[m],
            device_id={"section": 1 - section}, device_id_type=MESH,
        )
        copy.start()
        final.append((copy, out))
    for m, (copy, out) in enumerate(final):
        copy.wait_recv()
        out[...] = orecv[m]

    for pairs, sems in ((out_pairs, disp_s), (back_pairs, ret_s)):
        for j, (src, _) in enumerate(pairs):
            drain(src.at[pl.ds(0, experts - 1)], sems.at[j])
    for copy, _ in final:
        copy.wait_send()
    for t in range(3):
        for c in range(CHUNKS):
            for i in range(7):
                red_copy(t, c, i).wait_send()
                if t < 2:
                    gat_copy(t, c, i).wait_send()


ORDER = ("W0", "F0", "A0", "C0", "D0", "W1", "G0", "A1", "E0", "C1", "W2", "D1", "A2", "G1", "C2", "W3", "E1", "D2", "A3", "G2", "C3", "E2", "D3", "G3", "E3")


def solution(mesh):
    experts = mesh.shape["dev"]

    def shards(inf, rf, gf, inb, rb, gb, wg, wu, wd, sg, su):
        args = [v[0].T for v in (inf, inb, rf, rb, gf, gb)]
        args += [wg[0, 0], wu[0, 0], wd[0, 0].T, sg[0, 0], su[0, 0]]
        width, tokens = args[0].shape
        slots, hidden = args[9].shape
        rows, share = slots // CHUNKS, hidden // NODES
        vm = lambda *shape: pltpu.VMEM(shape, BF)
        both = [vm(experts, HEAD, 2 * width), vm(experts, TAIL, 2 * width)]
        dma = pltpu.SemaphoreType.DMA
        outs = pl.pallas_call(
            functools.partial(kernel, experts),
            out_shape=[jax.ShapeDtypeStruct((width, tokens), BF)] * 2,
            in_specs=[pl.BlockSpec(memory_space=pltpu.VMEM)] * 6 + [pl.BlockSpec(memory_space=pl.ANY)] * 5,
            out_specs=[pl.BlockSpec(memory_space=pltpu.VMEM)] * 2,
            scratch_shapes=[vm(width + 2 * PAD, hidden)] * 3
            + [vm(slots, hidden)] * 2
            + [pltpu.VMEM((slots, hidden), F32)] * 2
            + [vm(2, slots, 2 * tokens)]
            + both + both
            + [vm(3, CHUNKS, NODES, rows, share), vm(3, CHUNKS, 7, rows, share)]
            + [vm(3, CHUNKS, 3, rows, share), vm(2, CHUNKS, NODES, rows, share)]
            + both + both
            + [pltpu.VMEM((2, width + PAD, 2 * tokens), F32)]
            + [vm(2, width, tokens)] * 2
            + [dma((5,)), dma((2,)), dma((2,)), dma((CHUNKS, 2)), dma((2,)), dma((CHUNKS, 2))]
            + [dma((3, CHUNKS, 7))] * 2 + [dma((2, CHUNKS, 7))] * 2 + [dma((2,))] * 2,
            compiler_params=pltpu.CompilerParams(
                collective_id=0, has_side_effects=True, vmem_limit_bytes=56 * 1024 * 1024
            ),
            name="relay_layer",
        )(*args)
        return tuple(o.T[None] for o in outs)

    return jax.shard_map(
        shards,
        mesh=mesh,
        in_specs=(P("section", "dev", "node"), P("section", "dev", None), P("section", "dev", None)) * 2
        + (P("section", "dev", "node", None),) * 2
        + (P("section", "dev", None, "node"),)
        + (P("section", "dev", None, None),) * 2,
        out_specs=(P("section", "dev", "node"), P("section", "dev", "node")),
        check_vma=False,
    )
```

time: 138 us -> 120 us (0.87); the launches traced: 138 us -> 119 us
  Pallas kernels: 127 us -> 116 us
  local copies, waits for them, and re-layouts: 10.7 us -> 2.24 us
    pallas_call x1, Pallas kernels: 127 us -> 116 us  [shards(): pl.pallas_call(functools.partial(kernel, experts), out_shape=[jax.ShapeDt...]
    unnamed x23 -> x4, local copies, waits for them, and re-layouts: 10.7 us -> 2.24 us
where the time goes in v2:
time: 120 us; the launch traced here: 119 us
  Pallas kernels  116 us (97%)
  local copies, waits for them, and re-layouts  2.24 us (2%)
    pallas_call x1, Pallas kernels, shards(): pl.pallas_call(functools.partial(kernel, experts), out_shape=[jax.ShapeDt...  116 us

profile of v2, /device:TPU:1, one launch (start us, length us, event | category | flops | bytes accessed | tf_op | source)
XLA Modules:
  0.0 118.6 jit_solution(7077068423065412900)
XLA Ops:
  0.6 115.7 %relay_layer.1 = (bf16[448,128]{1,0:T(8,128)(2,1)}, bf16[448,128]{1,0:T(8,128)(2,1)}) custom-call(bf16[448,128]{1,0:T(8,128)(2,1)} %bitcast.38, bf16[448,128]{1,0:T(8,128)(2,1)} %bitcast.39, s32[2,128]{1,0:T(2,128)} %bitcast.40, s32[2,128]{1,0:T(2,128)} %bitcast.41, f32[2,128]{1,0:T(2,128)} %bitcast.42, f32[2,128]{1,0:T(2,128)} %bitcast.43, ...), custom_call_target="tpu_custom_call" | custom-call | tf_op jit(solution)/shard_map/relay_layer/pallas_call | solution.py:386
  116.4 0.0 copy-start
  116.4 1.6 %copy.15 = bf16[1,128,448]{1,2,0:T(8,128)(2,1)} copy(bf16[1,128,448]{1,2,0:T(8,128)(2,1)} %bitcast.37) | data formatting | bytes 229376
  118.0 0.0 copy-done
  118.0 0.6 copy.16
Async XLA Ops:
  116.4 1.6 %copy-start = (bf16[448,128]{1,0:T(8,128)(2,1)S(1)}, bf16[448,128]{1,0:T(8,128)(2,1)}, u32[]{:S(2)}) copy-start(bf16[448,128]{1,0:T(8,128)(2,1)} %get-tuple-element.5) | copy-start | bytes 344068

commit v3 on v2

--- a/solution.py
+++ b/solution.py
@@ -13,7 +13,7 @@
 CAPACITY = HEAD + TAIL
 NODES = 8
 LANES = 4
-GROUPS = ((0, 1, 11), (2, 10, 3), (6, 5, 7), (4, 8, 9))
+GROUPS = ((0, 1, 11), (4, 8, 9), (6, 5, 7), (2, 10, 3))
 PLANES = 12
 CHUNKS = len(GROUPS)
 DISTANCE = tuple(d for group in GROUPS for d in group)
@@ -50,7 +50,7 @@
 
 def kernel(
     experts, tokf, tokb, rf, rb, gf, gb, wg_h, wu_h, wd_h, sg_h, su_h, outf, outb,
-    wg, wu, wd, sg, su, for_gate, for_up, sel, sa, sb, ra, rb_in, part, got, sums, hid, ca, cb, da, db, acc, osend, orecv,
+    wg, wu, wd, sg, su, for_gate, for_up, sel, sa, sb, ra, rb_in, part, got, sums, hid, ca, cb, da, db, acc, osel, otokf, otokb, ogf, ogb,
     load_sem, own_sem, disp_s, disp_r, ret_s, ret_r, red_s, red_r, gat_s, gat_r, sec_s, sec_r,
 ):
     me = lax.axis_index("dev")
@@ -81,6 +81,10 @@
     def greet(k, carry):
         pl.semaphore_signal(
             barrier, inc=1, device_id={"dev": (me + k) % experts}, device_id_type=MESH
+        )
+        pl.semaphore_signal(
+            barrier, inc=1, device_id={"dev": (me + k) % experts, "section": 1 - section},
+            device_id_type=MESH,
         )
         return carry
 
@@ -150,7 +154,7 @@
             halves.append(dot(chosen[:, :tokens] + chosen[:, tokens:], wide[m], NT))
         split(widen(*halves), sa, sb, c)
 
-    def exchange(c, pairs, send, recv, to):
+    def exchange(c, pairs, send, recv, to, across):
         for i, dz in enumerate(GROUPS[c]):
             first = (c * len(GROUPS[c]) + i) * LANES
 
@@ -161,13 +165,13 @@
                         dst_ref=dst.at[first + dy],
                         send_sem=send.at[j],
                         recv_sem=recv.at[c, j],
-                        device_id={"dev": to(dz, dy)},
+                        device_id={"dev": to(dz, dy), "section": 1 - section if across else section},
                         device_id_type=MESH,
                     ).start()
                 return carry
 
-            lax.fori_loop(1 if dz == 0 else 0, LANES, go, 0)
-            if dz == 0:
+            lax.fori_loop(1 if dz == 0 and not across else 0, LANES, go, 0)
+            if dz == 0 and not across:
                 own = [
                     pltpu.make_async_copy(src.at[first], dst.at[first], own_sem.at[j])
                     for j, (src, dst) in enumerate(pairs)
@@ -177,9 +181,9 @@
                 for copy in own:
                     copy.wait()
 
-    def settle(c, pairs, recv):
+    def settle(c, pairs, recv, across):
         for j, (_, dst) in enumerate(pairs):
-            drain(dst.at[pl.ds(0, group - (0 in GROUPS[c]))], recv.at[c, j])
+            drain(dst.at[pl.ds(0, group - (0 in GROUPS[c] and not across))], recv.at[c, j])
 
     out_pairs = ((sa, ra), (sb, rb_in))
     back_pairs = ((ca, da), (cb, db))
@@ -187,8 +191,19 @@
     for c in range(CHUNKS):
         pack(c)
         if c == 0:
-            pl.semaphore_wait(barrier, experts - 1 + 4)
-        exchange(c, out_pairs, disp_s, disp_r, ahead)
+            pl.semaphore_wait(barrier, 2 * (experts - 1) + 4)
+        exchange(c, out_pairs, disp_s, disp_r, ahead, False)
+    handed = [
+        pltpu.make_async_remote_copy(
+            src_ref=src, dst_ref=dst, send_sem=sec_s.at[i], recv_sem=sec_r.at[i],
+            device_id={"section": 1 - section}, device_id_type=MESH,
+        )
+        for i, (src, dst) in enumerate(
+            ((sel, osel), (tokf, otokf), (tokb, otokb), (gf, ogf), (gb, ogb))
+        )
+    ]
+    for copy in handed:
+        copy.start()
 
     for load in loads[:3]:
         load.wait()
@@ -212,10 +227,10 @@
             for_up[:, span] = a * q
 
     def axes(t, c):
-        return (0, 1) if (t + c) % 2 == 0 else (1, 0)
-
-    def at(t, c, y, second, first):
-        return y * 4 + (second * 2 + first if axes(t, c)[0] == 0 else first * 2 + second)
+        return tuple("aby".index(axis) for axis in TRAVEL[c][t])
+
+    def at(t, c, third, second, first):
+        return sum(bit << d for bit, d in zip((first, second, third), axes(t, c)))
 
     def remote(src, dst, send, recv, to):
         return pltpu.make_async_remote_copy(
@@ -224,18 +239,18 @@
         )
 
     def red_copy(t, c, i):
-        d1, d2 = axes(t, c)
-        n1, n2, ny = 1 - bits[d1], bits[d2], bits[2]
+        d1, d2, d3 = axes(t, c)
+        n1, n2, ny = 1 - bits[d1], bits[d2], bits[d3]
         if i < 4:
             second = 1 - n2 if i < 2 else n2
             y = 1 - ny if i % 2 == 0 else ny
             src, to = part.at[t, c, at(t, c, y, second, n1)], d1
         else:
-            src, to = sums.at[t, c, i - 4], (d2 if i < 6 else 2)
+            src, to = sums.at[t, c, i - 4], (d2 if i < 6 else d3)
         return remote(src, got.at[t, c, i], red_s.at[t, c, i], red_r.at[t, c, i], to)
 
     def mine(t, c, y, second):
-        d1, _ = axes(t, c)
+        d1, _, _ = axes(t, c)
         return part[t, c, at(t, c, y, second, bits[d1])].astype(F32)
 
     def red_start(t, c):
@@ -243,33 +258,33 @@
             red_copy(t, c, i).start()
 
     def red_a(t, c, i):
-        _, d2 = axes(t, c)
+        _, d2, d3 = axes(t, c)
         red_copy(t, c, i).wait_recv()
-        y = 1 - bits[2] if i == 0 else bits[2]
+        y = 1 - bits[d3] if i == 0 else bits[d3]
         value = mine(t, c, y, 1 - bits[d2]) + got[t, c, i].astype(F32)
         sums[t, c, i] = value.astype(BF)
         red_copy(t, c, 4 + i).start()
 
     def red_c(t, c):
-        _, d2 = axes(t, c)
+        _, d2, d3 = axes(t, c)
         red_copy(t, c, 2).wait_recv()
         red_copy(t, c, 4).wait_recv()
-        value = mine(t, c, 1 - bits[2], bits[d2]) + got[t, c, 2].astype(F32)
+        value = mine(t, c, 1 - bits[d3], bits[d2]) + got[t, c, 2].astype(F32)
         sums[t, c, 2] = (value + got[t, c, 4].astype(F32)).astype(BF)
         red_copy(t, c, 6).start()
 
     def red_d(t, c):
-        _, d2 = axes(t, c)
+        _, d2, d3 = axes(t, c)
         for i in (3, 5, 6):
             red_copy(t, c, i).wait_recv()
-        value = mine(t, c, bits[2], bits[d2]) + got[t, c, 3].astype(F32)
+        value = mine(t, c, bits[d3], bits[d2]) + got[t, c, 3].astype(F32)
         return value + got[t, c, 5].astype(F32) + got[t, c, 6].astype(F32)
 
     def gat_copy(t, c, i):
-        d1, d2 = axes(t, c)
-        b1, b2, by = bits[d1], bits[d2], bits[2]
+        d1, d2, d3 = axes(t, c)
+        b1, b2, by = bits[d1], bits[d2], bits[d3]
         y, second, to = (
-            (by, b2, 2), (by, b2, d2), (1 - by, b2, d2),
+            (by, b2, d3), (by, b2, d2), (1 - by, b2, d2),
             (by, b2, d1), (1 - by, b2, d1), (by, 1 - b2, d1), (1 - by, 1 - b2, d1),
         )[i]
         ref = hid.at[t, c, at(t, c, y, second, b1)]
@@ -283,7 +298,7 @@
         return jnp.concatenate([hid[t, c, b] for b in range(NODES)], axis=1)
 
     def products(c):
-        settle(c, out_pairs, disp_r)
+        settle(c, out_pairs, disp_r, False)
         arrived = joined(ra, rb_in, c)
         for t, (value, w, zone) in enumerate(
             ((arrived[:, :512], wg, back), (arrived[:, :512], wu, back), (arrived[:, 384:], wd, front))
@@ -294,10 +309,9 @@
                 part[t, c, 2 * j + 1] = y[:, 128:]
             red_start(t, c)
 
-    def halve(c):
-        for i in range(2):
-            for t in range(3):
-                red_a(t, c, i)
+    def halve(c, i):
+        for t in range(3):
+            red_a(t, c, i)
 
     def settle_y(c):
         for t in range(3):
@@ -310,12 +324,11 @@
         hid[1, c, block] = red_d(2, c).astype(BF)
         gat_start(1, c)
 
-    def forward(c):
-        for wait, starts in ((0, (2, 4)), (1, (5,)), (2, (6,))):
-            for t in range(2):
-                gat_copy(t, c, wait).wait_recv()
-                for i in starts:
-                    gat_copy(t, c, i).start()
+    def forward(c, wait):
+        for t in range(2):
+            gat_copy(t, c, wait).wait_recv()
+            for i in ((2, 4), (5,), (6,))[wait]:
+                gat_copy(t, c, i).start()
 
     def finish(c):
         for t in range(2):
@@ -327,38 +340,41 @@
         second = dot((grad * for_gate[mine_rows, :]).astype(BF), wg[front, :], NT)
         second = second + dot((grad * for_up[mine_rows, :]).astype(BF), wu[front, :], NT)
         split(widen(first, second), ca, cb, c)
-        exchange(c, back_pairs, ret_s, ret_r, behind)
-
-    stages = {"W": products, "A": halve, "C": settle_y, "D": activate, "G": forward, "E": finish, "F": lambda _: factors()}
+        exchange(c, back_pairs, ret_s, ret_r, behind, True)
+
+    stages = {
+        "F": lambda _: factors(),
+        "W": products,
+        "A": lambda c: halve(c, 0),
+        "B": lambda c: halve(c, 1),
+        "C": settle_y,
+        "D": activate,
+        "G": lambda c: forward(c, 0),
+        "H": lambda c: forward(c, 1),
+        "I": lambda c: forward(c, 2),
+        "E": finish,
+    }
     for step in ORDER:
         stages[step[0]](int(step[1]))
 
+    for copy in handed:
+        copy.wait_recv()
     for c in range(CHUNKS):
-        settle(c, back_pairs, ret_r)
+        settle(c, back_pairs, ret_r, True)
         returned = joined(da, db, c)
         for m in range(2):
             value = returned[:, :512] if m == 0 else returned[:, 384:]
-            picked = dot(value, sel[m, c * rows : (c + 1) * rows, :], TN)
+            picked = dot(value, osel[m, c * rows : (c + 1) * rows, :], TN)
             acc[m] = picked if c == 0 else acc[m] + picked
-    final = []
-    for m, (tok, gates, out) in enumerate(((tokf, gf, outf), (tokb, gb, outb))):
+    for m, (tok, gates, out) in enumerate(((otokf, ogf, outf), (otokb, ogb, outb))):
         picked = acc[m, : 512 - PAD, :] if m == 0 else acc[m, PAD:, :]
         weighted = gates[0:1, :] * picked[:, :tokens] + gates[1:2, :] * picked[:, tokens:]
-        osend[m] = (tok[...].astype(F32) + weighted).astype(BF)
-        copy = pltpu.make_async_remote_copy(
-            src_ref=osend.at[m], dst_ref=orecv.at[m], send_sem=sec_s.at[m], recv_sem=sec_r.at[m],
-            device_id={"section": 1 - section}, device_id_type=MESH,
-        )
-        copy.start()
-        final.append((copy, out))
-    for m, (copy, out) in enumerate(final):
-        copy.wait_recv()
-        out[...] = orecv[m]
-
-    for pairs, sems in ((out_pairs, disp_s), (back_pairs, ret_s)):
+        out[...] = (tok[...].astype(F32) + weighted).astype(BF)
+
+    for pairs, sems, count in ((out_pairs, disp_s, experts - 1), (back_pairs, ret_s, experts)):
         for j, (src, _) in enumerate(pairs):
-            drain(src.at[pl.ds(0, experts - 1)], sems.at[j])
-    for copy, _ in final:
+            drain(src.at[pl.ds(0, count)], sems.at[j])
+    for copy in handed:
         copy.wait_send()
     for t in range(3):
         for c in range(CHUNKS):
@@ -368,7 +384,21 @@
                     gat_copy(t, c, i).wait_send()
 
 
-ORDER = ("W0", "F0", "A0", "C0", "D0", "W1", "G0", "A1", "E0", "C1", "W2", "D1", "A2", "G1", "C2", "W3", "E1", "D2", "A3", "G2", "C3", "E2", "D3", "G3", "E3")
+TRAVEL = (("aby", "bay", "aby"), ("bay", "aby", "bay"), ("aby", "bay", "aby"), ("bay", "aby", "bay"))
+ORDER = ("W0", "F0", "A0", "B0", "C0", "D0", "W1", "A1", "B1", "G0", "H0", "C1", "I0", "D1", "W2", "G1", "A2", "H1", "B2", "E0", "I1", "W3", "C2", "D2", "E1", "G2", "A3", "H2", "I2", "B3", "C3", "E2", "D3", "G3", "H3", "I3", "E3")
+
+
+def hand_over(first, second, first_out, second_out, first_buf, second_buf, sems):
+    pairs = ((first, first_buf, first_out), (second, second_buf, second_out))
+    into = [pltpu.make_async_copy(a, b, sems.at[i]) for i, (a, b, _) in enumerate(pairs)]
+    away = [pltpu.make_async_copy(b, c, sems.at[2 + i]) for i, (_, b, c) in enumerate(pairs)]
+    for copy in into:
+        copy.start()
+    for copy, onward in zip(into, away):
+        copy.wait()
+        onward.start()
+    for copy in away:
+        copy.wait()
 
 
 def solution(mesh):
@@ -397,14 +427,22 @@
             + [vm(3, CHUNKS, 3, rows, share), vm(2, CHUNKS, NODES, rows, share)]
             + both + both
             + [pltpu.VMEM((2, width + PAD, 2 * tokens), F32)]
-            + [vm(2, width, tokens)] * 2
+            + [vm(2, slots, 2 * tokens)] + [vm(width, tokens)] * 2 + [pltpu.VMEM((2, tokens), F32)] * 2
             + [dma((5,)), dma((2,)), dma((2,)), dma((CHUNKS, 2)), dma((2,)), dma((CHUNKS, 2))]
-            + [dma((3, CHUNKS, 7))] * 2 + [dma((2, CHUNKS, 7))] * 2 + [dma((2,))] * 2,
+            + [dma((3, CHUNKS, 7))] * 2 + [dma((2, CHUNKS, 7))] * 2 + [dma((5,))] * 2,
             compiler_params=pltpu.CompilerParams(
                 collective_id=0, has_side_effects=True, vmem_limit_bytes=56 * 1024 * 1024
             ),
             name="relay_layer",
         )(*args)
+        outs = pl.pallas_call(
+            hand_over,
+            out_shape=[jax.ShapeDtypeStruct((width, tokens), BF)] * 2,
+            in_specs=[pl.BlockSpec(memory_space=pl.ANY)] * 2,
+            out_specs=[pl.BlockSpec(memory_space=pl.ANY)] * 2,
+            scratch_shapes=[vm(width, tokens)] * 2 + [dma((4,))],
+            name="hand_over",
+        )(*outs)
         return tuple(o.T[None] for o in outs)
 
     return jax.shard_map(

time: 120 us -> 114 us (0.950)
  the two profiles are of different devices: /device:TPU:1 before, /device:TPU:65 now
where the time goes in v3:
time: 114 us
  Pallas kernels  113 us (99%)
    pallas_call x1, Pallas kernels, shards(): pl.pallas_call(functools.partial(kernel, experts), out_shape=[jax.ShapeDt...  112 us

profile of v3, /device:TPU:65, one launch (start us, length us, event | category | flops | bytes accessed | tf_op | source)
XLA Modules:
  0.0 113.8 jit_solution(13804769429894871549)
XLA Ops:
  0.6 111.5 %relay_layer.1 = (bf16[448,128]{1,0:T(8,128)(2,1)}, bf16[448,128]{1,0:T(8,128)(2,1)}) custom-call(bf16[448,128]{1,0:T(8,128)(2,1)} %bitcast.36, bf16[448,128]{1,0:T(8,128)(2,1)} %bitcast.37, s32[2,128]{1,0:T(2,128)} %bitcast.38, s32[2,128]{1,0:T(2,128)} %bitcast.39, f32[2,128]{1,0:T(2,128)} %bitcast.40, f32[2,128]{1,0:T(2,128)} %bitcast.41, ...), custom_call_target="tpu_custom_call" | custom-call | tf_op jit(solution)/shard_map/relay_layer/pallas_call | solution.py:416
  112.2 1.6 %hand_over.1 = (bf16[448,128]{1,0:T(8,128)(2,1)}, bf16[448,128]{1,0:T(8,128)(2,1)}) custom-call(bf16[448,128]{1,0:T(8,128)(2,1)} %get-tuple-element.6.first, bf16[448,128]{1,0:T(8,128)(2,1)} %get-tuple-element.7.second), custom_call_target="tpu_custom_call" | custom-call | tf_op jit(solution)/shard_map/hand_over/pallas_call | solution.py:438
